TPU v7x, 32 devices: a whole 2x2x4 slice. The times are simulated.
32 devices in a mesh: rows: 4 (over y, core), cols: 8 (over z, x).
Axes of the slice: x: 2, y: 2, z: 4, core: 2. Of those that a mesh axis runs over, the one named last changes fastest.
Arguments:
- features: bfloat16 [32768, 2048], P(('rows', 'cols')), may hold values from -6 to 6
- w_in: bfloat16 [2048, 1024], replicated, may hold values from -0.125 to 0.125
- w_out: bfloat16 [1024, 256], replicated, may hold values from -0.1875 to 0.1875
- item_ids: int32 [32768], P(('rows', 'cols')), may hold values from 0 to 32767, as said below
- item_counts: int32 [32768], P(('rows', 'cols')), may hold values from 0 to 65535
- owners: int32 [32768, 1], P(('rows', 'cols')), may hold values from 0 to 31; in each aligned block of 1024 rows (0 to 1023, 1024 to 2047, ...) at most 64 rows name the same one
- queries: bfloat16 [8192, 256], P('rows'), may hold values from -60 to 60
- positives: int32 [8192], replicated, may hold values from 0 to 32767, as said below
Outputs:
- cache_emb: bfloat16 [65536, 256], P(('rows', 'cols'))
- cache_ids: int32 [65536], P(('rows', 'cols'))
- query_loss: float32 [8192], P('rows')
Inputs may be any that keep to these rules, and one draw needn't show every extreme that they name: `item_ids`: all ids are different. `owners`: the items of one device name each owner at most 64 times; some owner is named exactly 64 times by one device's items. `positives`: each is the id of some item.
All inputs are finite; a program needn't handle non-finite values.
Results may differ from a plain program's by a relative error of at most 0.0049.
Values may be sent and summed in bfloat16 or wider, within the bound.
A program may use at most 128 MiB of HBM per device.

v0:
```python
import math

import jax
import jax.numpy as jnp
from jax import lax
from jax.sharding import PartitionSpec as P

FLOOR = -1e30


def merged(value, axis, combine):
    everything = jax.tree.map(lambda part: lax.all_gather(part, axis), value)
    first = jax.tree.map(lambda part: part[0], everything)

    def turn(k, so_far):
        return combine(so_far, jax.tree.map(lambda part: part[k], everything))

    return lax.fori_loop(1, lax.axis_size(axis), turn, first)


def combine(left_part, right_part):
    highest = jnp.maximum(left_part[0], right_part[0])
    summed = left_part[1] * jnp.exp(left_part[0] - highest) + right_part[1] * jnp.exp(
        right_part[0] - highest
    )
    return (highest, summed, left_part[2] + right_part[2])


def block_stats(q_rows, pos_rows, key_rows, key_ids, key_counts):
    score_scale = 4.0 / math.sqrt(key_rows.shape[1])
    log_q = jnp.log1p(key_counts.astype(jnp.float32))
    live_slot = key_ids >= 0
    raw_scores = (
        jnp.einsum("qe,ke->qk", q_rows, key_rows, preferred_element_type=jnp.float32) * score_scale
        - log_q[None, :]
    )
    masked = jnp.where(live_slot[None, :], raw_scores, FLOOR)
    highest = jnp.max(masked, axis=1)
    summed = jnp.sum(jnp.where(live_slot[None, :], jnp.exp(masked - highest[:, None]), 0.0), axis=1)
    positive_hit = jnp.sum(
        jnp.where(key_ids[None, :] == pos_rows[:, None], raw_scores, 0.0), axis=1
    )
    return (highest, summed, positive_hit)


def query_stats(q_all, pos_all, key_rows, key_ids, key_counts):
    query_count = q_all.shape[0]
    block_rows = min(query_count, 512)

    def score_block(inputs):
        return block_stats(inputs[0], inputs[1], key_rows, key_ids, key_counts)

    highest, summed, positive_hit = lax.map(
        score_block,
        (
            q_all.reshape(query_count // block_rows, block_rows, q_all.shape[1]),
            pos_all.reshape(query_count // block_rows, block_rows),
        ),
    )
    return (
        highest.reshape(query_count),
        summed.reshape(query_count),
        positive_hit.reshape(query_count),
    )


def local(features, w_in, w_out, item_ids, item_counts, owners, queries, positives):
    hidden = jnp.maximum(jnp.dot(features, w_in, preferred_element_type=jnp.float32), 0.0).astype(
        jnp.bfloat16
    )
    embedded = jnp.dot(hidden, w_out, preferred_element_type=jnp.float32).astype(jnp.bfloat16)
    n_rows = lax.axis_size("rows")
    n_cols = lax.axis_size("cols")
    devices = n_rows * n_cols
    items_dev = features.shape[0]
    capacity = 2 * items_dev // devices
    slot_count = devices * capacity
    owner_index = owners[:, 0]
    onehot = (owner_index[:, None] == jnp.arange(devices, dtype=jnp.int32)[None, :]).astype(
        jnp.int32
    )
    rank_within = jnp.sum((jnp.cumsum(onehot, axis=0) - onehot) * onehot, axis=1)
    slot_index = owner_index * capacity + rank_within
    send_emb = jnp.zeros((slot_count, embedded.shape[1]), jnp.bfloat16).at[slot_index].set(embedded)
    send_ids = jnp.full((slot_count,), -1, jnp.int32).at[slot_index].set(item_ids)
    send_counts = jnp.zeros((slot_count,), jnp.int32).at[slot_index].set(item_counts)
    pool_emb, pool_ids, pool_counts = (
        lax.all_to_all(send_emb, ("rows", "cols"), split_axis=0, concat_axis=0, tiled=True),
        lax.all_to_all(send_ids, ("rows", "cols"), split_axis=0, concat_axis=0, tiled=True),
        lax.all_to_all(send_counts, ("rows", "cols"), split_axis=0, concat_axis=0, tiled=True),
    )
    q_dev = queries.shape[0]
    row_index = lax.axis_index("rows")
    offset = row_index * q_dev
    pos_mine = lax.dynamic_slice_in_dim(positives, offset, q_dev)
    starting = (
        jnp.full((q_dev,), FLOOR, jnp.float32),
        jnp.zeros((q_dev,), jnp.float32),
        jnp.zeros((q_dev,), jnp.float32),
    )
    partials = combine(
        starting,
        query_stats(
            queries,
            pos_mine,
            lax.all_gather(pool_emb, "rows", axis=0, tiled=True),
            lax.all_gather(pool_ids, "rows", axis=0, tiled=True),
            lax.all_gather(pool_counts, "rows", axis=0, tiled=True),
        ),
    )
    highest, summed, positive_hit = merged(partials, "cols", combine)
    query_loss = highest + jnp.log(summed) - positive_hit
    return (pool_emb, pool_ids, query_loss)


def solution(mesh):
    placed = (
        P(("rows", "cols"), None),
        P(),
        P(),
        P(("rows", "cols")),
        P(("rows", "cols")),
        P(("rows", "cols"), None),
        P("rows", None),
        P(),
    )
    return jax.shard_map(
        local,
        mesh=mesh,
        in_specs=placed,
        out_specs=(P(("rows", "cols"), None), P(("rows", "cols")), P("rows")),
        check_vma=False,
    )
```

profile of v0, /device:TPU:0, one launch (start us, length us, event | category | flops | bytes accessed | tf_op | source)
XLA Modules:
  0.0 252.1 jit_solution(13637012453144365994)
XLA Ops:
  7.2 0.0 copy-start
  7.2 0.0 all-gather.5.cloned.1.call-start
  7.2 0.7 fusion.8
  8.0 9.0 %reduce-window.6 = s32[32,8,128]{2,1,0:T(8,128)S(1)} reduce-window(s32[32,8,128]{2,1,0:T(8,128)S(1)} %fusion.8, s32[]{:T(128)} %constant.96.clone.1), window={size=1x1x128 pad=0_0x0_0x127_0}, to_apply=%region_0.0 | reduce-window | flops 4161536 | bytes 262148 | tf_op jit(solution)/shard_map/reduce-window
  17.0 0.1 slice.23
  17.1 0.1 copy.13
  17.3 0.1 copy.14
  17.3 0.1 broadcast_add_fusion
  17.4 0.7 fusion.7
  18.2 0.7 compare_select_fusion
  18.9 0.0 copy-done
  18.9 8.6 %convolution_convert_fusion = bf16[1024,256]{1,0:T(8,128)(2,1)S(1)} fusion(bf16[1024,256]{1,0:T(8,128)(2,1)S(1)} %copy-done, bf16[1024,2048]{1,0:T(8,128)(2,1)} %param.12, bf16[2048,1024]{1,0:T(8,128)(2,1)} %param.13), kind=kOutput, calls=%fused_computation.17 | convolution fusion | flops 4834197504 | bytes 9437184 | tf_op jit(solution)/shard_map/dot_general | solution.py:71
  27.5 5.3 %scatter_custom_fusion = bf16[2048,256]{1,0:T(8,128)(2,1)S(1)} fusion(s32[1024]{0:T(1024)S(1)} %bitcast.116, bf16[1024,256]{1,0:T(8,128)(2,1)S(1)} %convolution_convert_fusion, bf16[]{:T(256)} %constant.94.clone.1), kind=kCustom, calls=%fused_computation.18 | custom fusion | bytes 1048578 | tf_op jit(solution)/shard_map/scatter | solution.py:84
  32.8 34.7 %all_to_all.36 = bf16[32,64,256]{2,1,0:T(8,128)(2,1)} all-to-all(bf16[32,64,256]{2,1,0:T(8,128)(2,1)S(1)} %bitcast.91), channel_id=1, replica_groups=mesh['rows'=4,'cols'=8] {'rows','cols'}, dimensions={0} | all-to-all | bytes 2097152 | tf_op jit(solution)/shard_map/all_to_all | solution.py:88
  67.5 0.0 all-gather.5.cloned.1.call-update
  67.5 4.5 %scatter_custom_fusion.1 = s32[2048]{0:T(1024)S(1)} fusion(s32[1024]{0:T(1024)S(1)} %bitcast.117, s32[1024]{0:T(1024)} %param.15, s32[]{:T(128)} %constant.99.clone.1), kind=kCustom, calls=%fused_computation.38 | custom fusion | bytes 8704 | tf_op jit(solution)/shard_map/scatter | solution.py:85
  72.0 0.7 all_to_all.27
  72.7 2.5 %all-to-all-start.1 = ((s32[32,64,1]{1,2,0:T(1,128)}), s32[32,64,1]{1,2,0:T(1,128)S(1)}, u32[]{:S(2)}, u32[]{:S(2)}) async-start(s32[32,64,1]{1,2,0:T(1,128)} %bitcast.17), calls=%async_computation.1 | async-start | bytes 32768 | tf_op jit(solution)/shard_map/all_to_all | solution.py:89
  75.3 4.5 %scatter_custom_fusion.2 = s32[2048]{0:T(1024)S(1)} fusion(s32[1024]{0:T(1024)S(1)} %bitcast.118, s32[1024]{0:T(1024)} %param.16, s32[]{:T(128)} %constant.96.clone.1), kind=kCustom, calls=%fused_computation.36 | custom fusion | bytes 8704 | tf_op jit(solution)/shard_map/scatter | solution.py:86
  79.8 0.7 all_to_all.30
  80.4 1.9 all-to-all-done.1
  82.3 3.9 %all-to-all-start.2 = ((s32[32,64,1]{1,2,0:T(1,128)}), s32[32,64,1]{1,2,0:T(1,128)S(1)}, u32[]{:S(2)}, u32[]{:S(2)}) async-start(s32[32,64,1]{1,2,0:T(1,128)} %bitcast.19), calls=%async_computation.2 | async-start | bytes 32768 | tf_op jit(solution)/shard_map/all_to_all | solution.py:90
  86.3 0.7 dynamic_slice.45
  87.0 0.5 broadcast.84
  87.5 0.7 reduce.6
  88.2 0.1 all_to_all.29
  88.3 0.0 copy-start.2
  88.3 5.1 %all-to-all-done.2 = s32[32,64,1]{1,2,0:T(1,128)S(1)} async-done(((s32[32,64,1]{1,2,0:T(1,128)}), s32[32,64,1]{1,2,0:T(1,128)S(1)}, u32[]{:S(2)}, u32[]{:S(2)}) %all-to-all-start.2) | async-done | bytes 8224 | tf_op jit(solution)/shard_map/all_to_all | solution.py:90
  93.4 0.7 reduce.7
  94.1 0.1 all_to_all.32
  94.2 5.4 %all_gather.20 = s32[8192]{0:T(1024)S(1)} all-gather(s32[2048]{0:T(1024)S(1)} %all_to_all.29), channel_id=1, replica_groups=mesh['rows'=4,'cols'=8] {'rows'}, dimensions={0}, use_global_device_ids=true | all-gather | bytes 40960 | tf_op jit(solution)/shard_map/all_gather | solution.py:107
  99.6 5.4 %all_gather.22 = s32[8192]{0:T(1024)S(1)} all-gather(s32[2048]{0:T(1024)S(1)} %all_to_all.32), channel_id=1, replica_groups=mesh['rows'=4,'cols'=8] {'rows'}, dimensions={0}, use_global_device_ids=true | all-gather | bytes 40960 | tf_op jit(solution)/shard_map/all_gather | solution.py:108
  104.9 0.0 all-gather.5.cloned.1.call-done
  105.0 0.0 copy-start.1
  105.0 0.0 copy-done.2
  105.0 46.1 %while.35 = (s32[]{:T(128)}, f32[4,512]{1,0:T(4,128)S(1)}, f32[4,512]{1,0:T(4,128)S(1)}, f32[4,512]{1,0:T(4,128)S(1)}, s32[8192]{0:T(1024)S(1)}, /*index=5*/bf16...) while((s32[]{:T(128)}, f32[4,512]{1,0:T(4,128)S(1)}, ...), condition=%wide.region_10.11_spmd, body=%wide.region_6.10_spmd.sunk | while | flops 2193627648 | bytes 38161020 | solution.py:53
  105.0 4.6 %select_reduce_fusion.5 = (f32[512]{0:T(512)S(1)}, f32[512,8192]{1,0:T(8,128)S(1)}) fusion(pred[8192]{0:T(1024)(128)(4,1)S(1)} %broadcast_compare_fusion.2, f32[8192]{0:T(1024)S(1)} %bitcast.109, bf16[8192,256]{1,0:T(8,128)(2,1)} %get-tuple-element.479, bf16[4,512,256]{2,1,0:T(8,128)(2,1)} %get-tuple-element.478, s32[]{:T(128)} %get-tuple-element.462), kind=kOutput, calls=%fused_computation.6.clone.1 | convolution fusion | flops 2164260352 | bytes 21277184 | tf_op jit(solution)/shard_map/while/body/eval_jaxpr/qe,ke->qk/dot_general | solution.py:34
  109.7 6.8 %select_reduce_fusion.6 = (f32[512]{0:T(512)S(1)}, f32[512]{0:T(512)S(1)}) fusion(f32[512,8192]{1,0:T(8,128)S(1)} %get-tuple-element.437, s32[8192]{0:T(1024)S(1)} %get-tuple-element.477, s32[512]{0:T(512)S(1)} %bitcast.102, f32[512]{0:T(512)S(1)} %get-tuple-element.436, pred[8192]{0:T(1024)(128)(4,1)S(1)} %broadcast_compare_fusion.2), kind=kLoop, calls=%fused_computation.3.clone.1 | loop fusion | flops 29359104 | bytes 16826368 | tf_op jit(solution)/shard_map/while/body/eval_jaxpr/reduce_sum | solution.py:40
  116.5 0.1 dynamic_update_slice.20
  116.5 0.1 dynamic_update_slice.19
  116.6 4.5 %select_reduce_fusion.5 = (f32[512]{0:T(512)S(1)}, f32[512,8192]{1,0:T(8,128)S(1)}) fusion(pred[8192]{0:T(1024)(128)(4,1)S(1)} %broadcast_compare_fusion.2, f32[8192]{0:T(1024)S(1)} %bitcast.109, bf16[8192,256]{1,0:T(8,128)(2,1)} %get-tuple-element.479, bf16[4,512,256]{2,1,0:T(8,128)(2,1)} %get-tuple-element.478, s32[]{:T(128)} %get-tuple-element.462), kind=kOutput, calls=%fused_computation.6.clone.1 | convolution fusion | flops 2164260352 | bytes 21277184 | tf_op jit(solution)/shard_map/while/body/eval_jaxpr/qe,ke->qk/dot_general | solution.py:34
  121.2 6.8 %select_reduce_fusion.6 = (f32[512]{0:T(512)S(1)}, f32[512]{0:T(512)S(1)}) fusion(f32[512,8192]{1,0:T(8,128)S(1)} %get-tuple-element.437, s32[8192]{0:T(1024)S(1)} %get-tuple-element.477, s32[512]{0:T(512)S(1)} %bitcast.102, f32[512]{0:T(512)S(1)} %get-tuple-element.436, pred[8192]{0:T(1024)(128)(4,1)S(1)} %broadcast_compare_fusion.2), kind=kLoop, calls=%fused_computation.3.clone.1 | loop fusion | flops 29359104 | bytes 16826368 | tf_op jit(solution)/shard_map/while/body/eval_jaxpr/reduce_sum | solution.py:40
  128.0 0.1 dynamic_update_slice.20
  128.0 0.1 dynamic_update_slice.19
  128.1 4.5 %select_reduce_fusion.5 = (f32[512]{0:T(512)S(1)}, f32[512,8192]{1,0:T(8,128)S(1)}) fusion(pred[8192]{0:T(1024)(128)(4,1)S(1)} %broadcast_compare_fusion.2, f32[8192]{0:T(1024)S(1)} %bitcast.109, bf16[8192,256]{1,0:T(8,128)(2,1)} %get-tuple-element.479, bf16[4,512,256]{2,1,0:T(8,128)(2,1)} %get-tuple-element.478, s32[]{:T(128)} %get-tuple-element.462), kind=kOutput, calls=%fused_computation.6.clone.1 | convolution fusion | flops 2164260352 | bytes 21277184 | tf_op jit(solution)/shard_map/while/body/eval_jaxpr/qe,ke->qk/dot_general | solution.py:34
  132.7 6.8 %select_reduce_fusion.6 = (f32[512]{0:T(512)S(1)}, f32[512]{0:T(512)S(1)}) fusion(f32[512,8192]{1,0:T(8,128)S(1)} %get-tuple-element.437, s32[8192]{0:T(1024)S(1)} %get-tuple-element.477, s32[512]{0:T(512)S(1)} %bitcast.102, f32[512]{0:T(512)S(1)} %get-tuple-element.436, pred[8192]{0:T(1024)(128)(4,1)S(1)} %broadcast_compare_fusion.2), kind=kLoop, calls=%fused_computation.3.clone.1 | loop fusion | flops 29359104 | bytes 16826368 | tf_op jit(solution)/shard_map/while/body/eval_jaxpr/reduce_sum | solution.py:40
  139.5 0.1 dynamic_update_slice.20
  139.5 0.1 dynamic_update_slice.19
  139.6 4.5 %select_reduce_fusion.5 = (f32[512]{0:T(512)S(1)}, f32[512,8192]{1,0:T(8,128)S(1)}) fusion(pred[8192]{0:T(1024)(128)(4,1)S(1)} %broadcast_compare_fusion.2, f32[8192]{0:T(1024)S(1)} %bitcast.109, bf16[8192,256]{1,0:T(8,128)(2,1)} %get-tuple-element.479, bf16[4,512,256]{2,1,0:T(8,128)(2,1)} %get-tuple-element.478, s32[]{:T(128)} %get-tuple-element.462), kind=kOutput, calls=%fused_computation.6.clone.1 | convolution fusion | flops 2164260352 | bytes 21277184 | tf_op jit(solution)/shard_map/while/body/eval_jaxpr/qe,ke->qk/dot_general | solution.py:34
  144.2 6.8 %select_reduce_fusion.6 = (f32[512]{0:T(512)S(1)}, f32[512]{0:T(512)S(1)}) fusion(f32[512,8192]{1,0:T(8,128)S(1)} %get-tuple-element.437, s32[8192]{0:T(1024)S(1)} %get-tuple-element.477, s32[512]{0:T(512)S(1)} %bitcast.102, f32[512]{0:T(512)S(1)} %get-tuple-element.436, pred[8192]{0:T(1024)(128)(4,1)S(1)} %broadcast_compare_fusion.2), kind=kLoop, calls=%fused_computation.3.clone.1 | loop fusion | flops 29359104 | bytes 16826368 | tf_op jit(solution)/shard_map/while/body/eval_jaxpr/reduce_sum | solution.py:40
  151.0 0.1 dynamic_update_slice.20
  151.0 0.1 dynamic_update_slice.19
  151.2 30.5 %all-gather = f32[8,1,2048]{2,1,0:T(1,128)S(1)} all-gather(f32[1,1,2048]{2,1,0:T(1,128)S(1)} %get-tuple-element.336), channel_id=1, replica_groups=mesh['rows'=4,'cols'=8] {'cols'}, dimensions={0}, use_global_device_ids=true | all-gather | bytes 73728 | tf_op jit(solution)/shard_map/all_gather | solution.py:12
  181.8 30.5 %all-gather.1 = f32[8,1,2048]{2,1,0:T(1,128)S(1)} all-gather(f32[1,1,2048]{2,1,0:T(1,128)S(1)} %get-tuple-element.335), channel_id=1, replica_groups=mesh['rows'=4,'cols'=8] {'cols'}, dimensions={0}, use_global_device_ids=true | all-gather | bytes 73728 | tf_op jit(solution)/shard_map/all_gather | solution.py:12
  212.4 30.5 %all-gather.2 = f32[8,1,2048]{2,1,0:T(1,128)S(1)} all-gather(f32[1,1,2048]{2,1,0:T(1,128)S(1)} %reshape.135), channel_id=1, replica_groups=mesh['rows'=4,'cols'=8] {'cols'}, dimensions={0}, use_global_device_ids=true | all-gather | bytes 73728 | tf_op jit(solution)/shard_map/all_gather | solution.py:12
  242.9 0.7 while.36
  243.6 0.6 add_subtract_fusion
  244.2 0.0 copy-done.1
  244.3 1.0 copy.58
  (57 shorter events, 0.8 us)
Async XLA Ops:
  7.2 11.7 %copy-start = (bf16[1024,256]{1,0:T(8,128)(2,1)S(1)}, bf16[1024,256]{1,0:T(8,128)(2,1)}, u32[]{:S(2)}) copy-start(bf16[1024,256]{1,0:T(8,128)(2,1)} %param.14) | copy-start | bytes 1572868
  7.2 97.8 %all-gather.5.cloned.1.call-start = ((), (), s32[]{:S(2)}) async-start(), calls=%async_computation.3 | async-start | bytes 5242880 | tf_op jit(solution)/shard_map/all_gather | solution.py:106
  72.7 9.6 %all-to-all-start.1 = ((s32[32,64,1]{1,2,0:T(1,128)}), s32[32,64,1]{1,2,0:T(1,128)S(1)}, u32[]{:S(2)}, u32[]{:S(2)}) async-start(s32[32,64,1]{1,2,0:T(1,128)} %bitcast.17), calls=%async_computation.1 | async-start | bytes 32768 | tf_op jit(solution)/shard_map/all_to_all | solution.py:89
  82.3 11.1 %all-to-all-start.2 = ((s32[32,64,1]{1,2,0:T(1,128)}), s32[32,64,1]{1,2,0:T(1,128)S(1)}, u32[]{:S(2)}, u32[]{:S(2)}) async-start(s32[32,64,1]{1,2,0:T(1,128)} %bitcast.19), calls=%async_computation.2 | async-start | bytes 32768 | tf_op jit(solution)/shard_map/all_to_all | solution.py:90
  88.3 16.7 %copy-start.2 = (s32[2048]{0:T(1024)}, s32[2048]{0:T(1024)S(1)}, u32[]{:S(2)}) copy-start(s32[2048]{0:T(1024)S(1)} %all_to_all.29) | copy-start | bytes 24580
  105.0 139.3 %copy-start.1 = (bf16[32,64,256]{2,1,0:T(8,128)(2,1)S(1)}, bf16[32,64,256]{2,1,0:T(8,128)(2,1)}, u32[]{:S(2)}) copy-start(bf16[32,64,256]{2,1,0:T(8,128)(2,1)} %all_to_all.36) | copy-start | bytes 3145732
Sparse Core Ops, SparseCore 0:
  67.7 32.8 all-gather.4
where the time goes:
time: 253 us; the launch traced here: 252 us
  blocking collectives  137 us (54%)
  other arithmetic  40.5 us (16%)
  matrix products  26.9 us (11%)
  local copies, waits for them, and re-layouts  19.2 us (8%)
  between operations  14.3 us (6%)
  waiting for transfers between devices  7.07 us (3%)
  starting transfers between devices  6.51 us (3%)
    all_gather x3, blocking collectives, merged(): everything = jax.tree.map(lambda part: lax.all_gather(part, axis), value)  91.6 us
    all_to_all x1, blocking collectives, local(): lax.all_to_all(send_emb, ('rows', 'cols'), split_axis=0, concat_axis=0, t...  34.7 us
    reduce_sum x4, other arithmetic, block_stats(): jnp.sum(jnp.where(key_ids[None, :] == pos_rows[:, None], raw_scores, 0.0)...  27 us
    dot_general x4, matrix products, block_stats(): jnp.einsum('qe,ke->qk', q_rows, key_rows, preferred_element_type=jnp.floa...  18.3 us
    another operation x6, other arithmetic  9.15 us
    dot_general x1, matrix products, local(): jnp.dot(hidden, w_out, preferred_element_type=jnp.float32)  8.63 us
    all_gather x1, blocking collectives, local(): lax.all_gather(pool_ids, 'rows', axis=0, tiled=True)  5.37 us
    all_gather x1, blocking collectives, local(): lax.all_gather(pool_counts, 'rows', axis=0, tiled=True)  5.35 us
  transfers between devices with their start and end apart: 3, of which 2 were waited for; matrix products, arithmetic and copies ran while one was open for 5% of the time, Pallas kernels for 0%

commit v1 on v0

v1 whole, which is shorter than its diff:
```python
import functools
import math

import jax
import jax.numpy as jnp
from jax import lax
from jax.experimental import pallas as pl
from jax.experimental.pallas import tpu as pltpu
from jax.sharding import PartitionSpec as P

MESH = pl.DeviceIdType.MESH
LANES = 128
LOW = -3.0e38
NT = (((1,), (1,)), ((), ()))


def kernel(
    n_rows, n_cols, cap, chunks, key_tile, query_tile,
    feat_hbm, w_in_hbm, w_out_hbm, ids_ref, counts_ref, owners_ref, q_hbm, pos_ref,
    cache_ref, cids_ref, loss_ref,
    feat, w_in, w_out, q, onehot, emb, aux, keyid, keylq, send, idsend, idrecv, pos,
    stats, parts, picked,
    load_sem, feat_sem, own_sem, aux_send, aux_recv, id_send, id_recv,
    emb_send, emb_recv, fwd_send, fwd_recv, a2a_send, a2a_recv, stat_send, stat_recv,
):
    n_dev = n_rows * n_cols
    n_y = n_rows // 2
    items, width = emb.shape[1] * emb.shape[2], emb.shape[3]
    chunk = items // chunks
    q_dev = q.shape[0]
    slots = n_dev * cap
    pack = LANES // cap
    row, col = lax.axis_index("rows"), lax.axis_index("cols")
    me = row * n_cols + col
    sib = row + 1 - 2 * lax.rem(row, 2)

    def place(index):
        return (lax.div(index, n_cols), lax.rem(index, n_cols))

    loads = [
        pltpu.make_async_copy(w_in_hbm, w_in, load_sem.at[0]),
        pltpu.make_async_copy(w_out_hbm, w_out, load_sem.at[1]),
        pltpu.make_async_copy(q_hbm, q, load_sem.at[2]),
    ]

    def feat_copy(i):
        return pltpu.make_async_copy(feat_hbm.at[i], feat.at[i], feat_sem.at[i])

    loads[0].start()
    feat_copy(0).start()
    loads[1].start()
    for i in range(1, chunks):
        feat_copy(i).start()
    loads[2].start()

    barrier = pltpu.get_barrier_semaphore()

    @pl.loop(1, n_dev)
    def _(k):
        pl.semaphore_signal(
            barrier, inc=1, device_id=place(lax.rem(me + k, n_dev)), device_id_type=MESH
        )

    aux[0] = jnp.zeros_like(aux[0])
    for i in range(items // LANES):
        lanes = slice(i * LANES, (i + 1) * LANES)
        aux[0, 0:1, lanes] = ids_ref[i : i + 1, :]
        aux[0, 1:2, lanes] = counts_ref[i : i + 1, :]
        aux[0, 2:3, lanes] = owners_ref[i : i + 1, :]
    for i in range(q_dev // LANES):
        pos[0:1, i * LANES : (i + 1) * LANES] = pos_ref[pl.ds(row * (q_dev // LANES) + i, 1), :]

    owner = aux[0, 2:3, :]
    named = (lax.broadcasted_iota(jnp.int32, (n_dev, items), 0) == owner).astype(jnp.float32)
    earlier = (
        lax.broadcasted_iota(jnp.int32, (items, items), 0)
        < lax.broadcasted_iota(jnp.int32, (items, items), 1)
    ).astype(jnp.float32).astype(jnp.bfloat16)
    before = jnp.dot(named.astype(jnp.bfloat16), earlier, preferred_element_type=jnp.float32)
    rank = jnp.sum(before * named, axis=0, keepdims=True).astype(jnp.int32)
    slot = owner * cap + rank

    value = aux[0, 0:1, :] + 1
    line = lax.broadcasted_iota(jnp.int32, (16, items), 0)
    digits = jnp.zeros((16, items), jnp.float32)
    for j in range(4):
        digit = lax.rem(lax.div(value, 256**j), 256).astype(jnp.float32)
        digits = jnp.where(line == j, digit, digits)
    digits = digits.astype(jnp.bfloat16)
    piece = onehot.shape[1]
    weight_line = lax.broadcasted_iota(jnp.int32, (16, piece), 0)
    weight = jnp.where(
        weight_line == 0, 1, jnp.where(weight_line == 1, 256, jnp.where(weight_line == 2, 65536, 0))
    ) + jnp.where(weight_line == 3, 1 << 24, 0)

    @pl.loop(0, slots // piece)
    def _(g):
        hot = (
            lax.broadcasted_iota(jnp.int32, (piece, items), 0) + g * piece == slot
        ).astype(jnp.float32).astype(jnp.bfloat16)
        onehot[g] = hot
        found = lax.dot_general(digits, hot, NT, preferred_element_type=jnp.float32)
        joined = jnp.sum(found.astype(jnp.int32) * weight, axis=0, keepdims=True) - 1
        for i in range(piece // LANES):
            idsend[g * (piece // LANES) + i] = jnp.broadcast_to(
                joined[:, i * LANES : (i + 1) * LANES], (8, LANES)
            )

    def spread(s):
        ids_row = aux[s, 0:1, :]
        lq_row = jnp.log(1.0 + aux[s, 1:2, :].astype(jnp.float32)) * (math.sqrt(width) / 4.0)
        for i in range(items // LANES):
            lanes = slice(i * LANES, (i + 1) * LANES)
            keyid[lanes, :] = jnp.broadcast_to(ids_row[:, lanes], (LANES, LANES)).T
            keylq[lanes, :] = jnp.broadcast_to(lq_row[:, lanes], (LANES, LANES)).T

    stats[0:1, :] = jnp.full((1, q_dev), LOW, jnp.float32)
    stats[1:3, :] = jnp.zeros((2, q_dev), jnp.float32)

    pl.semaphore_wait(barrier, n_dev - 1)

    def y_row(base, j):
        return lax.rem(base + n_rows - 2 * j, n_rows)

    aux_copies = []
    for s in range(1, n_rows):
        target = y_row(sib if s % 2 else row, s // 2)
        aux_copies.append(
            pltpu.make_async_remote_copy(
                src_ref=aux.at[0], dst_ref=aux.at[s], send_sem=aux_send.at[s],
                recv_sem=aux_recv.at[s], device_id=(target, col), device_id_type=MESH,
            )
        )
    for copy in aux_copies:
        copy.start()

    def id_copy(k):
        to = lax.rem(me + k, n_dev)
        return pltpu.make_async_remote_copy(
            src_ref=idsend.at[lax.div(to, pack)],
            dst_ref=idrecv.at[lax.div(me, pack), lax.rem(me, pack)],
            send_sem=id_send.at[k], recv_sem=id_recv.at[k],
            device_id=place(to), device_id_type=MESH,
        )

    @pl.loop(1, n_dev)
    def _(k):
        id_copy(k).start()

    def own_emb_copy(s, i):
        target = sib if s == 1 else y_row(row, s // 2)
        return pltpu.make_async_remote_copy(
            src_ref=emb.at[0, i], dst_ref=emb.at[s, i], send_sem=emb_send.at[s, i],
            recv_sem=emb_recv.at[s, i], device_id=(target, col), device_id_type=MESH,
        )

    def fwd_copy(s, i):
        return pltpu.make_async_remote_copy(
            src_ref=emb.at[s, i], dst_ref=emb.at[s + 1, i], send_sem=fwd_send.at[s, i],
            recv_sem=fwd_recv.at[s, i], device_id=(sib, col), device_id_type=MESH,
        )

    direct = [1] + [2 * j for j in range(1, n_y)]
    loads[0].wait()
    loads[1].wait()

    @pl.loop(0, chunks)
    def _(i):
        feat_copy(i).wait()
        hidden = jnp.maximum(
            jnp.dot(feat[i], w_in[...], preferred_element_type=jnp.float32), 0.0
        ).astype(jnp.bfloat16)
        emb[0, i] = jnp.dot(hidden, w_out[...], preferred_element_type=jnp.float32).astype(
            jnp.bfloat16
        )
        for s in reversed(direct):
            own_emb_copy(s, i).start()

    each = piece // cap

    @pl.loop(0, slots // piece)
    def _(g):
        total = jnp.zeros((piece, width), jnp.float32)
        for i in range(chunks):
            total = total + jnp.dot(
                onehot[g, :, i * chunk : (i + 1) * chunk], emb[0, i],
                preferred_element_type=jnp.float32,
            )
        rows_out = total.astype(jnp.bfloat16)
        for t in range(each):
            send[g * each + t] = rows_out[t * cap : (t + 1) * cap, :]

    def a2a_copy(k):
        to = lax.rem(me + k, n_dev)
        return pltpu.make_async_remote_copy(
            src_ref=send.at[to], dst_ref=cache_ref.at[me],
            send_sem=a2a_send.at[k], recv_sem=a2a_recv.at[k],
            device_id=place(to), device_id_type=MESH,
        )

    own_block = pltpu.make_async_copy(send.at[me], cache_ref.at[me], own_sem)

    @pl.loop(1, n_dev)
    def _(k):
        a2a_copy(k).start()

    own_block.start()
    loads[2].wait()

    steep = 4.0 / math.sqrt(width) * math.log2(math.e)

    def score(s, i):
        @pl.loop(0, chunk // key_tile)
        def _(t):
            base = i * chunk + t * key_tile
            keys = emb[s, i, pl.ds(t * key_tile, key_tile), :]
            wide = query_tile // LANES
            ident = jnp.concatenate([keyid[pl.ds(base, key_tile), :]] * wide, axis=1)
            lq = jnp.concatenate([keylq[pl.ds(base, key_tile), :]] * wide, axis=1)
            for u in range(q_dev // query_tile):
                lanes = slice(u * query_tile, (u + 1) * query_tile)
                raw = lax.dot_general(keys, q[lanes, :], NT, preferred_element_type=jnp.float32) - lq
                hit = jnp.sum(jnp.where(ident == pos[:, lanes], raw, 0.0), axis=0, keepdims=True)
                old = stats[0:1, lanes]
                top = jnp.maximum(old, jnp.max(raw, axis=0, keepdims=True))
                total = jnp.sum(jnp.exp2((raw - top) * steep), axis=0, keepdims=True)
                stats[0:1, lanes] = top
                stats[1:2, lanes] = stats[1:2, lanes] * jnp.exp2((old - top) * steep) + total
                stats[2:3, lanes] = stats[2:3, lanes] + hit

    spread(0)

    @pl.loop(0, chunks)
    def _(i):
        score(0, i)

    for s in range(1, n_rows):
        aux_copies[s - 1].wait()
        spread(s)

        @pl.loop(0, chunks)
        def _(i, s=s):
            if s == 1:
                own_emb_copy(1, i).wait()
            elif s % 2 == 0:
                own_emb_copy(s, i).wait()
                fwd_copy(s, i).start()
            else:
                fwd_copy(s - 1, i).wait()
            score(s, i)

    scale = 4.0 / math.sqrt(width)
    parts[0, 0:1, :] = stats[0:1, :] * scale + jnp.log(stats[1:2, :])
    parts[0, 1:2, :] = stats[2:3, :] * scale

    def stat_copy(k):
        return pltpu.make_async_remote_copy(
            src_ref=parts.at[0], dst_ref=parts.at[k],
            send_sem=stat_send.at[k], recv_sem=stat_recv.at[k],
            device_id=(row, lax.rem(col + k, n_cols)), device_id_type=MESH,
        )

    @pl.loop(1, n_cols)
    def _(k):
        stat_copy(k).start()

    idrecv[lax.div(me, pack), lax.rem(me, pack)] = idsend[lax.div(me, pack)]

    @pl.loop(1, n_dev)
    def _(k):
        id_copy(k).wait()

    lane = lax.broadcasted_iota(jnp.int32, (n_dev // pack, LANES), 1)
    result = jnp.zeros((n_dev // pack, LANES), jnp.int32)
    for j in range(pack):
        shift = lax.rem(j + pack - lax.rem(me, pack), pack) * cap
        for g in range(n_dev // pack):
            picked[g : g + 1, :] = idrecv[g, j, 0:1, :]
        turned = pltpu.roll(picked[...], shift, 1)
        result = jnp.where(lax.div(lane, cap) == j, turned, result)
    cids_ref[...] = result

    @pl.loop(1, n_cols)
    def _(k):
        stat_copy(k).wait()

    highest = parts[0, 0:1, :]
    for k in range(1, n_cols):
        highest = jnp.maximum(highest, parts[k, 0:1, :])
    summed = jnp.zeros_like(highest)
    positive = jnp.zeros_like(highest)
    for k in range(n_cols):
        summed = summed + jnp.exp(parts[k, 0:1, :] - highest)
        positive = positive + parts[k, 1:2, :]
    loss = highest + jnp.log(summed) - positive
    for i in range(q_dev // LANES):
        loss_ref[i : i + 1, :] = loss[:, i * LANES : (i + 1) * LANES]

    @pl.loop(1, n_dev)
    def _(k):
        a2a_copy(k).wait()

    own_block.wait()


def local(n_rows, n_cols, features, w_in, w_out, item_ids, item_counts, owners, queries, positives):
    n_dev = n_rows * n_cols
    items, wide = features.shape
    hid, width = w_out.shape
    cap = 2 * items // n_dev
    slots = n_dev * cap
    pack = LANES // cap
    q_dev = queries.shape[0]
    chunks = 4
    piece = 256
    bf16, i32, f32 = jnp.bfloat16, jnp.int32, jnp.float32
    hbm = pl.BlockSpec(memory_space=pl.ANY)
    vmem = pl.BlockSpec(memory_space=pltpu.VMEM)
    dma = pltpu.SemaphoreType.DMA
    cache, ids, loss = pl.pallas_call(
        functools.partial(kernel, n_rows, n_cols, cap, chunks, 256, 512),
        out_shape=(
            jax.ShapeDtypeStruct((n_dev, cap, width), bf16),
            jax.ShapeDtypeStruct((slots // LANES, LANES), i32),
            jax.ShapeDtypeStruct((q_dev // LANES, LANES), f32),
        ),
        in_specs=[hbm, hbm, hbm, vmem, vmem, vmem, hbm, vmem],
        out_specs=(hbm, vmem, vmem),
        scratch_shapes=[
            pltpu.VMEM((chunks, items // chunks, wide), bf16),
            pltpu.VMEM(w_in.shape, bf16),
            pltpu.VMEM(w_out.shape, bf16),
            pltpu.VMEM(queries.shape, bf16),
            pltpu.VMEM((slots // piece, piece, items), bf16),
            pltpu.VMEM((n_rows, chunks, items // chunks, width), bf16),
            pltpu.VMEM((n_rows, 8, items), i32),
            pltpu.VMEM((items, LANES), i32),
            pltpu.VMEM((items, LANES), f32),
            pltpu.VMEM((n_dev, cap, width), bf16),
            pltpu.VMEM((slots // LANES, 8, LANES), i32),
            pltpu.VMEM((n_dev // pack, pack, 8, LANES), i32),
            pltpu.VMEM((1, q_dev), i32),
            pltpu.VMEM((8, q_dev), f32),
            pltpu.VMEM((n_cols, 2, q_dev), f32),
            pltpu.VMEM((n_dev // pack, LANES), i32),
            dma((3,)), dma((chunks,)), dma,
            dma((n_rows,)), dma((n_rows,)),
            dma((n_dev,)), dma((n_dev,)),
            dma((n_rows, chunks)), dma((n_rows, chunks)),
            dma((n_rows, chunks)), dma((n_rows, chunks)),
            dma((n_dev,)), dma((n_dev,)),
            dma((n_cols,)), dma((n_cols,)),
        ],
        compiler_params=pltpu.CompilerParams(
            collective_id=0, has_side_effects=True, vmem_limit_bytes=56 * 1024 * 1024
        ),
        name="refresh",
    )(
        features.reshape(chunks, items // chunks, wide),
        w_in,
        w_out,
        item_ids.reshape(items // LANES, LANES),
        item_counts.reshape(items // LANES, LANES),
        owners.reshape(items // LANES, LANES),
        queries,
        positives.reshape(positives.shape[0] // LANES, LANES),
    )
    return cache.reshape(slots, width), ids.reshape(slots), loss.reshape(q_dev)


def solution(mesh):
    placed = (
        P(("rows", "cols"), None),
        P(),
        P(),
        P(("rows", "cols")),
        P(("rows", "cols")),
        P(("rows", "cols"), None),
        P("rows", None),
        P(),
    )
    return jax.shard_map(
        functools.partial(local, mesh.shape["rows"], mesh.shape["cols"]),
        mesh=mesh,
        in_specs=placed,
        out_specs=(P(("rows", "cols"), None), P(("rows", "cols")), P("rows")),
        check_vma=False,
    )
```

time: 253 us -> 52.1 us (0.21)
  blocking collectives: 137 us -> 0 us
  Pallas kernels: 0 us -> 46.3 us
  other arithmetic: 40.5 us -> 0 us
  matrix products: 26.9 us -> 0 us
  local copies, waits for them, and re-layouts: 19.2 us -> 4.85 us
  between operations: 14.3 us -> 0.64 us
  waiting for transfers between devices: 7.07 us -> 0 us
  starting transfers between devices: 6.51 us -> 0 us
    all_gather x5 -> x0, blocking collectives: 102 us -> none  [the longest x3 91.6 us: merged(): everything = jax.tree.map(lambda part: lax.all_gather(part, axis), value)]
    pallas_call x0 -> x1, Pallas kernels: none -> 46.3 us  [local(): pl.pallas_call(functools.partial(kernel, n_rows, n_cols, cap, chunks, 256...]
    all_to_all x1 -> x0, blocking collectives: 34.7 us -> none  [local(): lax.all_to_all(send_emb, ('rows', 'cols'), split_axis=0, concat_axis=0, t...]
    reduce_sum x5 -> x0, other arithmetic: 27.7 us -> none  [the longest x4 27 us: block_stats(): jnp.sum(jnp.where(key_ids[None, :] == pos_rows[:, None], raw_scores, 0.0)...]
    dot_general x5 -> x0, matrix products: 26.9 us -> none  [the longest x4 18.3 us: block_stats(): jnp.einsum('qe,ke->qk', q_rows, key_rows, preferred_element_type=jnp.floa...]
    scatter x3 -> x0, local copies, waits for them, and re-layouts: 14.2 us -> none  [the longest x1 5.28 us: local(): jnp.zeros((slot_count, embedded.shape[1]), jnp.bfloat16).at[slot_index]]
    another operation x6 -> x0, other arithmetic: 9.15 us -> none
    all_to_all x2 -> x0, waiting for transfers between devices: 7.03 us -> none  [the longest x1 5.12 us: local(): lax.all_to_all(send_counts, ('rows', 'cols'), split_axis=0, concat_axis=0...]
  transfers between devices with their start and end apart: 3 -> 0, of which waited for: 2 -> 0; matrix products, arithmetic and copies ran while one was open for 5% -> 0% of each run, Pallas kernels for 0% -> 0%
where the time goes in v1:
time: 52.1 us; the launch traced here: 51.8 us
  Pallas kernels  46.3 us (89%)
  local copies, waits for them, and re-layouts  4.85 us (9%)
  between operations  0.64 us (1%)
    pallas_call x1, Pallas kernels, local(): pl.pallas_call(functools.partial(kernel, n_rows, n_cols, cap, chunks, 256...  46.3 us
    unnamed x3, local copies, waits for them, and re-layouts  4.85 us

profile of v1, /device:TPU:0, one launch (start us, length us, event | category | flops | bytes accessed | tf_op | source)
XLA Modules:
  0.0 51.8 jit_solution(12512322155624829229)
XLA Ops:
  0.6 46.3 %refresh.1 = (bf16[32,64,256]{2,1,0:T(8,128)(2,1)}, s32[16,128]{1,0:T(8,128)}, f32[16,128]{1,0:T(8,128)}) custom-call(bf16[4,256,2048]{2,1,0:T(8,128)(2,1)} %bitcast.8, bf16[2048,1024]{1,0:T(8,128)(2,1)} %w_in_hbm.1, bf16[1024,256]{1,0:T(8,128)(2,1)} %w_out_hbm.1, s32[8,128]{1,0:T(8,128)} %bitcast.13, s32[8,128]{1,0:T(8,128)} %bitcast.14, ...), custom_call_target="tpu_custom_call" | custom-call | tf_op jit(solution)/shard_map/refresh/pallas_call | solution.py:320
  46.9 2.3 %copy.14 = bf16[2048,256]{1,0:T(8,128)(2,1)} copy(bf16[2048,256]{1,0:T(8,128)(2,1)} %bitcast.9) | data formatting | bytes 2097152
  49.2 1.3 %copy.15 = s32[2048]{0:T(1024)} copy(s32[2048]{0:T(1024)} %bitcast.12) | data formatting | bytes 16384
  50.5 1.3 %copy.16 = f32[2048]{0:T(1024)} copy(f32[2048]{0:T(1024)} %bitcast.11) | data formatting | bytes 16384

commit v2 on v1

--- a/solution.py
+++ b/solution.py
@@ -15,10 +15,10 @@
 
 
 def kernel(
-    n_rows, n_cols, cap, chunks, key_tile, query_tile,
+    n_rows, n_cols, cap, chunks, piece, key_tile, query_tile,
     feat_hbm, w_in_hbm, w_out_hbm, ids_ref, counts_ref, owners_ref, q_hbm, pos_ref,
     cache_ref, cids_ref, loss_ref,
-    feat, w_in, w_out, q, onehot, emb, aux, keyid, keylq, send, idsend, idrecv, pos,
+    feat, w_in, w_out, q, emb, aux, keyid, keylq, send, idsend, idrecv, pos,
     stats, parts, picked,
     load_sem, feat_sem, own_sem, aux_send, aux_recv, id_send, id_recv,
     emb_send, emb_recv, fwd_send, fwd_recv, a2a_send, a2a_recv, stat_send, stat_recv,
@@ -68,7 +68,9 @@
         aux[0, 1:2, lanes] = counts_ref[i : i + 1, :]
         aux[0, 2:3, lanes] = owners_ref[i : i + 1, :]
     for i in range(q_dev // LANES):
-        pos[0:1, i * LANES : (i + 1) * LANES] = pos_ref[pl.ds(row * (q_dev // LANES) + i, 1), :]
+        pos[:, i * LANES : (i + 1) * LANES] = jnp.broadcast_to(
+            pos_ref[pl.ds(row * (q_dev // LANES) + i, 1), :], (8, LANES)
+        )
 
     owner = aux[0, 2:3, :]
     named = (lax.broadcasted_iota(jnp.int32, (n_dev, items), 0) == owner).astype(jnp.float32)
@@ -87,24 +89,10 @@
         digit = lax.rem(lax.div(value, 256**j), 256).astype(jnp.float32)
         digits = jnp.where(line == j, digit, digits)
     digits = digits.astype(jnp.bfloat16)
-    piece = onehot.shape[1]
     weight_line = lax.broadcasted_iota(jnp.int32, (16, piece), 0)
     weight = jnp.where(
         weight_line == 0, 1, jnp.where(weight_line == 1, 256, jnp.where(weight_line == 2, 65536, 0))
     ) + jnp.where(weight_line == 3, 1 << 24, 0)
-
-    @pl.loop(0, slots // piece)
-    def _(g):
-        hot = (
-            lax.broadcasted_iota(jnp.int32, (piece, items), 0) + g * piece == slot
-        ).astype(jnp.float32).astype(jnp.bfloat16)
-        onehot[g] = hot
-        found = lax.dot_general(digits, hot, NT, preferred_element_type=jnp.float32)
-        joined = jnp.sum(found.astype(jnp.int32) * weight, axis=0, keepdims=True) - 1
-        for i in range(piece // LANES):
-            idsend[g * (piece // LANES) + i] = jnp.broadcast_to(
-                joined[:, i * LANES : (i + 1) * LANES], (8, LANES)
-            )
 
     def spread(s):
         ids_row = aux[s, 0:1, :]
@@ -114,10 +102,10 @@
             keyid[lanes, :] = jnp.broadcast_to(ids_row[:, lanes], (LANES, LANES)).T
             keylq[lanes, :] = jnp.broadcast_to(lq_row[:, lanes], (LANES, LANES)).T
 
-    stats[0:1, :] = jnp.full((1, q_dev), LOW, jnp.float32)
-    stats[1:3, :] = jnp.zeros((2, q_dev), jnp.float32)
-
-    pl.semaphore_wait(barrier, n_dev - 1)
+    stats[0] = jnp.full((8, q_dev), LOW, jnp.float32)
+    stats[1] = jnp.zeros((8, q_dev), jnp.float32)
+    stats[2] = jnp.zeros((8, q_dev), jnp.float32)
+    spread(0)
 
     def y_row(base, j):
         return lax.rem(base + n_rows - 2 * j, n_rows)
@@ -131,9 +119,6 @@
                 recv_sem=aux_recv.at[s], device_id=(target, col), device_id_type=MESH,
             )
         )
-    for copy in aux_copies:
-        copy.start()
-
     def id_copy(k):
         to = lax.rem(me + k, n_dev)
         return pltpu.make_async_remote_copy(
@@ -143,10 +128,6 @@
             device_id=place(to), device_id_type=MESH,
         )
 
-    @pl.loop(1, n_dev)
-    def _(k):
-        id_copy(k).start()
-
     def own_emb_copy(s, i):
         target = sib if s == 1 else y_row(row, s // 2)
         return pltpu.make_async_remote_copy(
@@ -164,8 +145,7 @@
     loads[0].wait()
     loads[1].wait()
 
-    @pl.loop(0, chunks)
-    def _(i):
+    def tower(i):
         feat_copy(i).wait()
         hidden = jnp.maximum(
             jnp.dot(feat[i], w_in[...], preferred_element_type=jnp.float32), 0.0
@@ -173,22 +153,30 @@
         emb[0, i] = jnp.dot(hidden, w_out[...], preferred_element_type=jnp.float32).astype(
             jnp.bfloat16
         )
+
+    def share(i):
         for s in reversed(direct):
             own_emb_copy(s, i).start()
 
-    each = piece // cap
-
-    @pl.loop(0, slots // piece)
-    def _(g):
-        total = jnp.zeros((piece, width), jnp.float32)
-        for i in range(chunks):
-            total = total + jnp.dot(
-                onehot[g, :, i * chunk : (i + 1) * chunk], emb[0, i],
-                preferred_element_type=jnp.float32,
-            )
-        rows_out = total.astype(jnp.bfloat16)
-        for t in range(each):
-            send[g * each + t] = rows_out[t * cap : (t + 1) * cap, :]
+    head = chunks // 2
+
+    @pl.loop(0, head)
+    def _(i):
+        tower(i)
+
+    pl.semaphore_wait(barrier, n_dev - 1)
+
+    @pl.loop(0, head)
+    def _(i):
+        share(i)
+
+    for copy in aux_copies:
+        copy.start()
+
+    @pl.loop(head, chunks)
+    def _(i):
+        tower(i)
+        share(i)
 
     def a2a_copy(k):
         to = lax.rem(me + k, n_dev)
@@ -199,12 +187,43 @@
         )
 
     own_block = pltpu.make_async_copy(send.at[me], cache_ref.at[me], own_sem)
+    each = piece // cap
+    groups = slots // piece
+    first = lax.div(me, each) + 1
+
+    @pl.loop(0, groups)
+    def _(step):
+        g = lax.rem(first + step, groups)
+        hot = (
+            lax.broadcasted_iota(jnp.int32, (piece, items), 0) + g * piece == slot
+        ).astype(jnp.float32).astype(jnp.bfloat16)
+        total = jnp.zeros((piece, width), jnp.float32)
+        for i in range(chunks):
+            total = total + jnp.dot(
+                hot[:, i * chunk : (i + 1) * chunk], emb[0, i], preferred_element_type=jnp.float32
+            )
+        rows_out = total.astype(jnp.bfloat16)
+        for t in range(each):
+            send[g * each + t] = rows_out[t * cap : (t + 1) * cap, :]
+        found = lax.dot_general(digits, hot, NT, preferred_element_type=jnp.float32)
+        joined = jnp.sum(found.astype(jnp.int32) * weight, axis=0, keepdims=True) - 1
+        for i in range(piece // LANES):
+            idsend[g * (piece // LANES) + i] = joined[:, i * LANES : (i + 1) * LANES]
+
+        @pl.loop(0, each)
+        def _(t):
+            k = lax.rem(g * each + t + n_dev - me, n_dev)
+
+            @pl.when(k > 0)
+            def _():
+                a2a_copy(k).start()
+
+    own_block.start()
 
     @pl.loop(1, n_dev)
     def _(k):
-        a2a_copy(k).start()
-
-    own_block.start()
+        id_copy(k).start()
+
     loads[2].wait()
 
     steep = 4.0 / math.sqrt(width) * math.log2(math.e)
@@ -217,18 +236,18 @@
             wide = query_tile // LANES
             ident = jnp.concatenate([keyid[pl.ds(base, key_tile), :]] * wide, axis=1)
             lq = jnp.concatenate([keylq[pl.ds(base, key_tile), :]] * wide, axis=1)
+            ident = ident.reshape(key_tile // 8, 8, query_tile)
             for u in range(q_dev // query_tile):
                 lanes = slice(u * query_tile, (u + 1) * query_tile)
                 raw = lax.dot_general(keys, q[lanes, :], NT, preferred_element_type=jnp.float32) - lq
-                hit = jnp.sum(jnp.where(ident == pos[:, lanes], raw, 0.0), axis=0, keepdims=True)
-                old = stats[0:1, lanes]
-                top = jnp.maximum(old, jnp.max(raw, axis=0, keepdims=True))
-                total = jnp.sum(jnp.exp2((raw - top) * steep), axis=0, keepdims=True)
-                stats[0:1, lanes] = top
-                stats[1:2, lanes] = stats[1:2, lanes] * jnp.exp2((old - top) * steep) + total
-                stats[2:3, lanes] = stats[2:3, lanes] + hit
-
-    spread(0)
+                raw = raw.reshape(key_tile // 8, 8, query_tile)
+                hit = jnp.sum(jnp.where(ident == pos[:, lanes][None], raw, 0.0), axis=0)
+                old = stats[0, :, lanes]
+                top = jnp.maximum(old, jnp.max(raw, axis=0))
+                total = jnp.sum(jnp.exp2((raw - top[None]) * steep), axis=0)
+                stats[0, :, lanes] = top
+                stats[1, :, lanes] = stats[1, :, lanes] * jnp.exp2((old - top) * steep) + total
+                stats[2, :, lanes] = stats[2, :, lanes] + hit
 
     @pl.loop(0, chunks)
     def _(i):
@@ -250,8 +269,10 @@
             score(s, i)
 
     scale = 4.0 / math.sqrt(width)
-    parts[0, 0:1, :] = stats[0:1, :] * scale + jnp.log(stats[1:2, :])
-    parts[0, 1:2, :] = stats[2:3, :] * scale
+    best = jnp.max(stats[0], axis=0, keepdims=True)
+    mass = jnp.sum(stats[1] * jnp.exp2((stats[0] - best) * steep), axis=0, keepdims=True)
+    parts[0, 0:1, :] = best * scale + jnp.log(mass)
+    parts[0, 1:2, :] = jnp.sum(stats[2], axis=0, keepdims=True) * scale
 
     def stat_copy(k):
         return pltpu.make_async_remote_copy(
@@ -301,6 +322,23 @@
         a2a_copy(k).wait()
 
     own_block.wait()
+
+
+def settle(*refs):
+    sources, targets, held, sems = refs[0:3], refs[3:6], refs[6:9], refs[9]
+    inward = [
+        pltpu.make_async_copy(a, h, sems.at[i]) for i, (a, h) in enumerate(zip(sources, held))
+    ]
+    outward = [
+        pltpu.make_async_copy(h, b, sems.at[3 + i]) for i, (h, b) in enumerate(zip(held, targets))
+    ]
+    for copy in inward:
+        copy.start()
+    for copy, onward in zip(inward[::-1], outward[::-1]):
+        copy.wait()
+        onward.start()
+    for onward in outward:
+        onward.wait()
 
 
 def local(n_rows, n_cols, features, w_in, w_out, item_ids, item_counts, owners, queries, positives):
@@ -318,7 +356,7 @@
     vmem = pl.BlockSpec(memory_space=pltpu.VMEM)
     dma = pltpu.SemaphoreType.DMA
     cache, ids, loss = pl.pallas_call(
-        functools.partial(kernel, n_rows, n_cols, cap, chunks, 256, 512),
+        functools.partial(kernel, n_rows, n_cols, cap, chunks, piece, 256, 512),
         out_shape=(
             jax.ShapeDtypeStruct((n_dev, cap, width), bf16),
             jax.ShapeDtypeStruct((slots // LANES, LANES), i32),
@@ -331,16 +369,15 @@
             pltpu.VMEM(w_in.shape, bf16),
             pltpu.VMEM(w_out.shape, bf16),
             pltpu.VMEM(queries.shape, bf16),
-            pltpu.VMEM((slots // piece, piece, items), bf16),
             pltpu.VMEM((n_rows, chunks, items // chunks, width), bf16),
             pltpu.VMEM((n_rows, 8, items), i32),
             pltpu.VMEM((items, LANES), i32),
             pltpu.VMEM((items, LANES), f32),
             pltpu.VMEM((n_dev, cap, width), bf16),
-            pltpu.VMEM((slots // LANES, 8, LANES), i32),
-            pltpu.VMEM((n_dev // pack, pack, 8, LANES), i32),
-            pltpu.VMEM((1, q_dev), i32),
-            pltpu.VMEM((8, q_dev), f32),
+            pltpu.VMEM((slots // LANES, 1, LANES), i32),
+            pltpu.VMEM((n_dev // pack, pack, 1, LANES), i32),
+            pltpu.VMEM((8, q_dev), i32),
+            pltpu.VMEM((3, 8, q_dev), f32),
             pltpu.VMEM((n_cols, 2, q_dev), f32),
             pltpu.VMEM((n_dev // pack, LANES), i32),
             dma((3,)), dma((chunks,)), dma,
@@ -365,6 +402,15 @@
         queries,
         positives.reshape(positives.shape[0] // LANES, LANES),
     )
+    cache, ids, loss = pl.pallas_call(
+        settle,
+        out_shape=tuple(jax.ShapeDtypeStruct(x.shape, x.dtype) for x in (cache, ids, loss)),
+        in_specs=[hbm] * 3,
+        out_specs=(hbm,) * 3,
+        scratch_shapes=[pltpu.VMEM(x.shape, x.dtype) for x in (cache, ids, loss)] + [dma((6,))],
+        compiler_params=pltpu.CompilerParams(vmem_limit_bytes=60 * 1024 * 1024),
+        name="settle",
+    )(cache, ids, loss)
     return cache.reshape(slots, width), ids.reshape(slots), loss.reshape(q_dev)
 
 

time: 52.1 us -> 49.4 us (0.948)
  local copies, waits for them, and re-layouts: 4.85 us -> 0 us
  Pallas kernels: 46.3 us -> 48.5 us
    unnamed x3 -> x0, local copies, waits for them, and re-layouts: 4.85 us -> none
    pallas_call x1 -> x2, Pallas kernels: 46.3 us -> 48.5 us  [the longest x1 46.3 us: local(): pl.pallas_call(functools.partial(kernel, n_rows, n_cols, cap, chunks, pie...]
where the time goes in v2:
time: 49.4 us; the launch traced here: 49.2 us
  Pallas kernels  48.5 us (98%)
  between operations  0.64 us (1%)
    pallas_call x1, Pallas kernels, local(): pl.pallas_call(functools.partial(kernel, n_rows, n_cols, cap, chunks, pie...  46.3 us
    pallas_call x1, Pallas kernels, local(): pl.pallas_call(settle, out_shape=tuple((jax.ShapeDtypeStruct(x.shape, x.d...  2.25 us

profile of v2, /device:TPU:0, one launch (start us, length us, event | category | flops | bytes accessed | tf_op | source)
XLA Modules:
  0.0 49.2 jit_solution(14965203710812333298)
XLA Ops:
  0.6 46.3 %refresh.1 = (bf16[32,64,256]{2,1,0:T(8,128)(2,1)}, s32[16,128]{1,0:T(8,128)}, f32[16,128]{1,0:T(8,128)}) custom-call(bf16[4,256,2048]{2,1,0:T(8,128)(2,1)} %bitcast.8, bf16[2048,1024]{1,0:T(8,128)(2,1)} %w_in_hbm.1, bf16[1024,256]{1,0:T(8,128)(2,1)} %w_out_hbm.1, s32[8,128]{1,0:T(8,128)} %bitcast.10, s32[8,128]{1,0:T(8,128)} %bitcast.11, ...), custom_call_target="tpu_custom_call" | custom-call | tf_op jit(solution)/shard_map/refresh/pallas_call | solution.py:358
  46.9 2.3 %settle.1 = (bf16[32,64,256]{2,1,0:T(8,128)(2,1)}, s32[16,128]{1,0:T(8,128)}, f32[16,128]{1,0:T(8,128)}) custom-call(bf16[32,64,256]{2,1,0:T(8,128)(2,1)} %get-tuple-element.9.refs_0_, s32[16,128]{1,0:T(8,128)} %get-tuple-element.10.refs_1_, f32[16,128]{1,0:T(8,128)} %get-tuple-element.11.refs_2_), custom_call_target="tpu_custom_call" | custom-call | tf_op jit(solution)/shard_map/settle/pallas_call | solution.py:405
